TPU v7x, 256 devices: a whole 4x4x8 slice. The times are simulated.
256 devices in a mesh: wide: 32 (over y, x, core), narrow: 8 (over z).
Axes of the slice: x: 4, y: 4, z: 8, core: 2. Of those that a mesh axis runs over, the one named last changes fastest.
Arguments:
- features: bfloat16 [1024, 16384], P('wide', 'narrow'), may hold values from -6 to 6
- queries: bfloat16 [2048, 16384], P('wide', 'narrow'), may hold values from -6 to 6
- damping: float32 [16384], P('wide'), may hold values from 0.25 to 4
Outputs:
- kernel: float32 [16384, 16384], P('wide', 'narrow')
- factor: float32 [16384, 256], P('wide')
- scores: float32 [2048, 1024], P('wide', 'narrow')
All inputs are finite; a program needn't handle non-finite values.
Results may differ from a plain program's by a relative error of at most 0.0003.
Values may be sent and summed in bfloat16 or wider, within the bound.
A program may use at most 64 MiB of HBM per device.

v0:
```python
import math

import jax
import jax.numpy as jnp
from jax import lax
from jax.sharding import PartitionSpec as P

P_SIZE = 16384
PANEL = 128
PANELS = 2


def laid_out(pieces, dim):
    pieces = jnp.moveaxis(pieces, 0, dim)
    shape = pieces.shape
    return pieces.reshape(*shape[:dim], shape[dim] * shape[dim + 1], *shape[dim + 2 :])


def copy_for_each(x, axis):
    copies = jnp.broadcast_to(x, (lax.axis_size(axis), *x.shape))
    return lax.all_to_all(copies, axis, split_axis=0, concat_axis=0, tiled=True)


def collect(x, axis, dim):
    return laid_out(copy_for_each(x, axis), dim)


def in_blocks(x, dim, size):
    before, after = (x.shape[:dim], x.shape[dim + 1 :])
    return jnp.moveaxis(x.reshape(*before, size, -1, *after), dim, 0)


def sent_and_summed(x, axis, dim):
    size = lax.axis_size(axis)
    pieces = lax.all_to_all(in_blocks(x, dim, size), axis, 0, 0, tiled=True)
    return jnp.sum(pieces, axis=0)


def broadcast(x, axis, root):
    return lax.dynamic_index_in_dim(lax.all_gather(x, axis), root, 0, keepdims=False)


def on_device(features, queries, damping):
    rows_here = damping.shape[0]
    cols_here = queries.shape[1]
    slab_total = features.shape[0] * lax.axis_size("wide")
    wide_pos = lax.axis_index("wide")
    narrow_pos = lax.axis_index("narrow")
    contract_rows = (((0,), (0,)), ((), ()))
    contract_cols = (((1,), (1,)), ((), ()))
    full_width = collect(features, "narrow", 1)
    row_features = lax.all_to_all(full_width, "wide", split_axis=1, concat_axis=0, tiled=True)
    slab_columns = lax.all_gather(features, "wide", axis=0, tiled=True)
    products = lax.dot_general(
        row_features, slab_columns, contract_rows, preferred_element_type=jnp.float32
    )
    partial_value = lax.dot_general(
        queries, slab_columns, contract_cols, preferred_element_type=jnp.float32
    )
    scores = sent_and_summed(partial_value, "narrow", 1) * (1.0 / math.sqrt(P_SIZE))
    row_ids = wide_pos * rows_here + lax.broadcasted_iota(jnp.int32, (rows_here, 1), 0)
    col_ids = narrow_pos * cols_here + lax.broadcasted_iota(jnp.int32, (1, cols_here), 1)
    kernel_block = products / slab_total + jnp.where(
        row_ids == col_ids, damping[:, None], jnp.float32(0.0)
    )
    factors = []
    for panel_index in range(PANELS):
        offset = panel_index * PANEL
        column_root = offset // cols_here
        row_root = offset // rows_here
        col_shift = offset % cols_here
        row_shift = offset % rows_here
        panel_columns = broadcast(
            kernel_block[:, col_shift : col_shift + PANEL], "narrow", column_root
        )
        pivot_block = broadcast(panel_columns[row_shift : row_shift + PANEL], "wide", row_root)
        pivot_factor = jnp.linalg.cholesky(pivot_block)
        lower_rows = lax.linalg.triangular_solve(
            pivot_factor, panel_columns, left_side=False, lower=True, transpose_a=True
        )
        per_group = cols_here // rows_here
        pieces = []
        for member in range(per_group):
            pieces.append(broadcast(lower_rows, "wide", narrow_pos * per_group + member))
        lower_cols = jnp.concatenate(pieces, axis=0)
        kernel_block = kernel_block - jnp.dot(
            lower_rows,
            lower_cols.T,
            precision=lax.Precision.HIGHEST,
            preferred_element_type=jnp.float32,
        )
        boundary = offset + PANEL
        kernel_block = jnp.where(
            (row_ids < boundary) | (col_ids < boundary), jnp.zeros_like(kernel_block), kernel_block
        )
        factors.append(lower_rows)
    return (kernel_block, jnp.concatenate(factors, axis=1), scores)


def solution(mesh):
    return jax.shard_map(
        on_device,
        mesh=mesh,
        in_specs=(P("wide", "narrow"), P("wide", "narrow"), P("wide")),
        out_specs=(P("wide", "narrow"), P("wide", None), P("wide", "narrow")),
        check_vma=False,
    )
```

profile of v0, /device:TPU:1, one launch (start us, length us, event | category | flops | bytes accessed | tf_op | source)
XLA Modules:
  0.0 475.3 jit_solution(2787711246564530403)
XLA Ops:
  7.9 1.0 broadcast_in_dim.15
  8.9 36.2 %all_to_all.29 = bf16[8,32,2048]{2,1,0:T(8,128)(2,1)S(1)} all-to-all(bf16[8,32,2048]{2,1,0:T(8,128)(2,1)S(1)} %broadcast_in_dim.15), channel_id=1, replica_groups=mesh['wide'=32,'narrow'=8] {'narrow'}, dimensions={0} | all-to-all | bytes 2097152 | tf_op jit(solution)/shard_map/all_to_all | solution.py:21
  46.4 1.5 copy.16
  47.9 9.4 %all-to-all-start.1 = ((bf16[32,32,512]{2,0,1:T(8,128)(2,1)}), bf16[32,32,512]{2,0,1:T(8,128)(2,1)S(1)}, u32[]{:S(2)}, u32[]{:S(2)}) async-start(bf16[32,32,512]{2,0,1:T(8,128)(2,1)} %copy.16), calls=%async_computation.1 | async-start | bytes 2097152 | tf_op jit(solution)/shard_map/all_to_all | solution.py:52
  57.4 18.8 %all-to-all-done.1 = bf16[32,32,512]{2,0,1:T(8,128)(2,1)S(1)} async-done(((bf16[32,32,512]{2,0,1:T(8,128)(2,1)}), bf16[32,32,512]{2,0,1:T(8,128)(2,1)S(1)}, u32[]{:S(2)}, u32[]{:S(2)}) %all-to-all-start.1) | async-done | bytes 1048608 | tf_op jit(solution)/shard_map/all_to_all | solution.py:52
  76.2 5.0 %select_add_fusion = f32[512,2048]{1,0:T(8,128)S(1)} fusion(bf16[1024,512]{1,0:T(8,128)(2,1)S(1)} %bitcast.87, bf16[1024,2048]{1,0:T(8,128)(2,1)} %all-gather.12.cloned.1.call-done, f32[512]{0:T(512)S(1)} %copy-done.7, s32[2048]{0:T(1024)S(1)} %iota_add_fusion, s32[512]{0:T(512)S(1)} %iota_add_fusion.1), kind=kOutput, calls=%fused_computation.2 | convolution fusion | flops 2151677952 | bytes 9449472 | tf_op jit(solution)/shard_map/dot_general | solution.py:54
  81.2 2.0 copy-done.3
  84.0 33.5 %all-gather.18.cloned.1.call-done = f32[4096,128]{1,0:T(8,128)} async-done(((f32[512,128]{1,0:T(8,128)}), f32[4096,128]{1,0:T(8,128)}) %all-gather.18.cloned.1.call-update) | async-done | bytes 2097168 | tf_op jit(solution)/shard_map/all_gather | solution.py:40
  117.6 1.5 slice.33
  119.1 53.3 %all-gather.14.cloned.1.call-done = f32[32,128,128]{2,1,0:T(8,128)} async-done(((f32[1,128,128]{2,1,0:T(8,128)}), f32[32,128,128]{2,1,0:T(8,128)}) %all-gather.14.cloned.1.call-update) | async-done | bytes 2097168 | tf_op jit(solution)/shard_map/all_gather | solution.py:40
  174.3 11.7 %cholesky.44 = f32[128,128]{1,0:T(8,128)S(1)} custom-call(f32[128,128]{1,0:T(8,128)S(1)} %fusion.19), custom_call_target="Cholesky" | custom-call | tf_op jit(solution)/shard_map/jit(cholesky)/cholesky | solution.py:77
  187.3 9.8 %custom-call.6 = f32[1,128,128]{1,2,0:T(8,128)S(1)} custom-call(f32[1,128,128]{2,1,0:T(8,128)S(1)} %fusion.16), custom_call_target="InvertDiagBlocksLowerTriangular" | custom-call | tf_op jit(solution)/shard_map/triangular_solve/custom-call.0 | solution.py:78
  197.1 2.1 convolution_bitcast_fusion.2
  199.5 57.1 %all-gather.20.cloned.1.call-done = f32[16384,128]{0,1:T(8,128)} async-done(((f32[512,128]{0,1:T(8,128)}), f32[16384,128]{0,1:T(8,128)}) %all-gather.20.cloned.1.call-update) | async-done | bytes 8388624 | tf_op jit(solution)/shard_map/all_gather | solution.py:40
  256.6 9.9 %copy.36 = f32[16,8,32,512]{3,2,1,0:T(8,128)S(1)} copy(f32[16,8,32,512]{3,1,2,0:T(8,128)} %bitcast.80) | data formatting | bytes 16777216
  266.5 1.2 constant_dynamic-slice_fusion.7
  268.7 4.0 subtract_select_fusion.1
  272.8 2.0 copy-done.1
  275.6 36.0 %all-gather.22.cloned.1.call-done = f32[4096,128]{1,0:T(8,128)} async-done(((f32[512,128]{1,0:T(8,128)}), f32[4096,128]{1,0:T(8,128)}) %all-gather.22.cloned.1.call-update) | async-done | bytes 2097168 | tf_op jit(solution)/shard_map/all_gather | solution.py:40
  311.6 1.5 slice.36
  313.4 53.0 %all-gather.16.cloned.1.call-done = f32[32,128,128]{2,1,0:T(8,128)} async-done(((f32[1,128,128]{2,1,0:T(8,128)}), f32[32,128,128]{2,1,0:T(8,128)}) %all-gather.16.cloned.1.call-update) | async-done | bytes 2097168 | tf_op jit(solution)/shard_map/all_gather | solution.py:40
  368.1 11.7 %cholesky.55 = f32[128,128]{1,0:T(8,128)S(1)} custom-call(f32[128,128]{1,0:T(8,128)S(1)} %fusion.18), custom_call_target="Cholesky" | custom-call | tf_op jit(solution)/shard_map/jit(cholesky)/cholesky | solution.py:77
  381.2 9.8 %custom-call.7 = f32[1,128,128]{1,2,0:T(8,128)S(1)} custom-call(f32[1,128,128]{2,1,0:T(8,128)S(1)} %fusion.17), custom_call_target="InvertDiagBlocksLowerTriangular" | custom-call | tf_op jit(solution)/shard_map/triangular_solve/custom-call.0 | solution.py:78
  391.0 2.1 convolution_bitcast_fusion.1
  393.2 3.6 convolution_bitcast_fusion
  397.5 7.0 %all-to-all-start.2 = ((f32[8,64,128]{2,1,0:T(8,128)}), f32[8,64,128]{2,1,0:T(8,128)S(1)}, u32[]{:S(2)}, u32[]{:S(2)}) async-start(f32[8,64,128]{2,1,0:T(8,128)} %bitcast.73), calls=%async_computation.2 | async-start | bytes 524288 | tf_op jit(solution)/shard_map/all_to_all | solution.py:35
  404.5 11.6 %all-to-all-done.2 = f32[8,64,128]{2,1,0:T(8,128)S(1)} async-done(((f32[8,64,128]{2,1,0:T(8,128)}), f32[8,64,128]{2,1,0:T(8,128)S(1)}, u32[]{:S(2)}, u32[]{:S(2)}) %all-to-all-start.2) | async-done | bytes 262176 | tf_op jit(solution)/shard_map/all_to_all | solution.py:35
  416.9 1.0 copy.22
  417.9 32.7 %all-gather.24.cloned.1.call-done = f32[16384,128]{0,1:T(8,128)} async-done(((f32[512,128]{0,1:T(8,128)}), f32[16384,128]{0,1:T(8,128)}) %all-gather.24.cloned.1.call-update) | async-done | bytes 8388624 | tf_op jit(solution)/shard_map/all_gather | solution.py:40
  450.5 9.9 %copy.37 = f32[16,8,32,512]{3,2,1,0:T(8,128)S(1)} copy(f32[16,8,32,512]{3,1,2,0:T(8,128)} %bitcast.81) | data formatting | bytes 16777216
  460.4 1.2 constant_dynamic-slice_fusion.3
  462.6 5.5 %subtract_select_fusion = f32[512,2048]{1,0:T(8,128)} fusion(f32[512,2048]{1,0:T(8,128)S(1)} %copy-done.2, f32[512,128]{0,1:T(8,128)S(1)} %copy-done.6, pred[2048]{0:T(1024)(128)(4,1)S(1)} %fusion.23, pred[512]{0:T(512)(128)(4,1)S(1)} %fusion.25, f32[512,128]{0,1:T(8,128)S(1)} %bitcast.84, f32[512,128]{0,1:T(8,128)S(1)} %bitcast.85, ...), kind=kOutput, calls=%fused_computation | convolution fusion | flops 1614544896 | bytes 9701888 | tf_op jit(solution)/shard_map/dot_general | solution.py:86
  (61 shorter events, 13.9 us)
Async XLA Ops:
  7.2 386.0 %copy-start = (bf16[64,2048]{1,0:T(8,128)(2,1)S(1)}, bf16[64,2048]{1,0:T(8,128)(2,1)}, u32[]{:S(2)}) copy-start(bf16[64,2048]{1,0:T(8,128)(2,1)} %param.7) | copy-start | bytes 786436
  7.2 69.1 %all-gather.12.cloned.1.call-start = ((), (), s32[]{:S(2)}) async-start(), calls=%async_computation.3 | async-start | bytes 4325376 | tf_op jit(solution)/shard_map/all_gather | solution.py:53
  45.1 31.2 %copy-start.7 = (f32[512]{0:T(512)S(1)}, f32[512]{0:T(512)}, u32[]{:S(2)}) copy-start(f32[512]{0:T(512)} %param.8) | copy-start | bytes 6148
  47.9 28.3 %all-to-all-start.1 = ((bf16[32,32,512]{2,0,1:T(8,128)(2,1)}), bf16[32,32,512]{2,0,1:T(8,128)(2,1)S(1)}, u32[]{:S(2)}, u32[]{:S(2)}) async-start(bf16[32,32,512]{2,0,1:T(8,128)(2,1)} %copy.16), calls=%async_computation.1 | async-start | bytes 2097152 | tf_op jit(solution)/shard_map/all_to_all | solution.py:52
  57.3 60.3 %all-gather.18.cloned.1.call-start = ((), (), s32[]{:S(2)}) async-start(), calls=%async_computation.6 | async-start | bytes 2359296 | tf_op jit(solution)/shard_map/all_gather | solution.py:40
  81.2 2.0 copy-start.3
  84.0 88.5 %all-gather.14.cloned.1.call-start = ((), (), s32[]{:S(2)}) async-start(), calls=%async_computation.4 | async-start | bytes 2162688 | tf_op jit(solution)/shard_map/all_gather | solution.py:40
  119.1 137.5 %all-gather.20.cloned.1.call-start = ((), (), s32[]{:S(2)}) async-start(), calls=%async_computation.7 | async-start | bytes 8650752 | tf_op jit(solution)/shard_map/all_gather | solution.py:40
  199.2 112.4 %all-gather.22.cloned.1.call-start = ((), (), s32[]{:S(2)}) async-start(), calls=%async_computation.8 | async-start | bytes 2359296 | tf_op jit(solution)/shard_map/all_gather | solution.py:40
  256.6 11.2 %copy-start.5 = (f32[512,128]{0,1:T(8,128)S(1)}, f32[512,128]{0,1:T(8,128)}, u32[]{:S(2)}) copy-start(f32[512,128]{0,1:T(8,128)} %convolution_bitcast_fusion.2) | copy-start | bytes 786436
  266.5 2.2 copy-start.4
  272.8 2.0 copy-start.1
  275.5 90.8 %all-gather.16.cloned.1.call-start = ((), (), s32[]{:S(2)}) async-start(), calls=%async_computation.5 | async-start | bytes 2162688 | tf_op jit(solution)/shard_map/all_gather | solution.py:40
  313.1 137.4 %all-gather.24.cloned.1.call-start = ((), (), s32[]{:S(2)}) async-start(), calls=%async_computation.9 | async-start | bytes 8650752 | tf_op jit(solution)/shard_map/all_gather | solution.py:40
  393.1 23.7 %copy-start.6 = (f32[512,128]{0,1:T(8,128)S(1)}, f32[512,128]{0,1:T(8,128)}, u32[]{:S(2)}) copy-start(f32[512,128]{0,1:T(8,128)} %convolution_bitcast_fusion.1) | copy-start | bytes 786436
  397.5 18.7 %all-to-all-start.2 = ((f32[8,64,128]{2,1,0:T(8,128)}), f32[8,64,128]{2,1,0:T(8,128)S(1)}, u32[]{:S(2)}, u32[]{:S(2)}) async-start(f32[8,64,128]{2,1,0:T(8,128)} %bitcast.73), calls=%async_computation.2 | async-start | bytes 524288 | tf_op jit(solution)/shard_map/all_to_all | solution.py:35
  460.4 2.2 copy-start.2
Sparse Core Ops, SparseCore 0:
  10.5 60.5 all-gather.11
  84.1 33.4 all-gather.17
  120.7 51.7 all-gather.13
  199.4 57.2 all-gather.19
  275.7 35.8 all-gather.21
  314.6 51.7 all-gather.15
  393.3 57.2 all-gather.23
where the time goes:
time: 484 us; the launch traced here: 475 us
  waiting for transfers between devices  297 us (61%)
  other arithmetic  48.1 us (10%)
  local copies, waits for them, and re-layouts  39.9 us (8%)
  blocking collectives  36.2 us (7%)
  matrix products  22.3 us (5%)
  starting transfers between devices  17.1 us (4%)
  between operations  14.9 us (3%)
    all_gather x6, waiting for transfers between devices, broadcast(): lax.all_gather(x, axis)  266 us
    all_to_all x1, blocking collectives, copy_for_each(): return lax.all_to_all(copies, axis, split_axis=0, concat_axis=0, tiled=True)  36.2 us
    unnamed x27, local copies, waits for them, and re-layouts  26.9 us
    another operation x6, other arithmetic, on_device(): pivot_factor = jnp.linalg.cholesky(pivot_block)  24.8 us
    another operation x4, other arithmetic, on_device(): lax.linalg.triangular_solve(pivot_factor, panel_columns, left_side=False,...  20.9 us
    all_to_all x1, waiting for transfers between devices, on_device(): lax.all_to_all(full_width, 'wide', split_axis=1, concat_axis=0, tiled=True)  18.8 us
    all_to_all x1, waiting for transfers between devices, sent_and_summed(): pieces = lax.all_to_all(in_blocks(x, dim, size), axis, 0, 0, tiled=True)  11.6 us
  transfers between devices with their start and end apart: 9, of which 8 were waited for; matrix products, arithmetic and copies ran while one was open for 2% of the time, Pallas kernels for 0%

commit v1 on v0

v1 whole, which is shorter than its diff:
```python
import functools
import math

import jax
import jax.numpy as jnp
from jax import lax
from jax.experimental import pallas as pl
from jax.experimental.pallas import tpu as pltpu
from jax.sharding import PartitionSpec as P

P_SIZE = 16384
PIV = 256
SLAB = 1024
MESH = pl.DeviceIdType.MESH
F32 = jnp.float32
BF16 = jnp.bfloat16

ORDER = (
    (0, 0), (3, 0), (1, 0), (0, 3), (0, 1), (2, 0), (3, 3), (1, 3),
    (3, 1), (1, 1), (2, 3), (2, 1), (0, 2), (3, 2), (1, 2), (2, 2),
)
RELAYED = 10
LAST_STEP = 25


def _table(values, p):
    out = jnp.int32(0)
    for k, v in enumerate(values):
        if v:
            out = out + jnp.where(p == k, jnp.int32(v), jnp.int32(0))
    return out


def gather_kernel(
    feat, qry, damp, fj, fi, fp, dp, sc,
    part, inbox,
    ag_recv, ag_send, pt_recv, pt_send, z_recv, z_send, fpz_recv, fpz_send,
    fp_recv, fp_send, fpp_recv, fpp_send, d_recv, d_send, rs_recv, rs_send, local,
):
    w = lax.axis_index("wide")
    z = lax.axis_index("narrow")
    c = lax.rem(w, 2)
    x = lax.rem(lax.div(w, 2), 4)
    y = lax.div(w, 8)

    def spot(da, db, core):
        px = lax.rem(x + da + core * (db - da), 4)
        py = lax.rem(y + db + core * (da - db), 4)
        return px, py

    def dev(da, db):
        px, py = spot(da, db, c)
        return ((py * 4 + px) * 2 + c, z)

    def row(da, db, core):
        px, py = spot(da, db, core)
        return pl.multiple_of((core * 16 + py * 4 + px) * 32, 32)

    partner = (w + 1 - 2 * c, z)
    own = row(0, 0, c)

    def rcopy(src, dst, ssem, rsem, to):
        return pltpu.make_async_remote_copy(
            src_ref=src, dst_ref=dst, send_sem=ssem, recv_sem=rsem, device_id=to, device_id_type=MESH
        )

    barrier = pltpu.get_barrier_semaphore()

    @pl.loop(1, 32)
    def _(k):
        pl.semaphore_signal(barrier, inc=1, device_id=(lax.rem(w + k, 32), z), device_id_type=MESH)

    @pl.loop(1, 8)
    def _(k):
        pl.semaphore_signal(barrier, inc=1, device_id=(w, lax.rem(z + k, 8)), device_id_type=MESH)

    pl.semaphore_wait(barrier, 38)

    def fpz(k):
        return rcopy(
            feat.at[:, pl.ds(0, PIV)], fp.at[pl.ds(own, 32), :], fpz_send.at[k], fpz_recv,
            (w, lax.rem(z + k, 8)),
        )

    fp_own = pltpu.make_async_copy(feat.at[:, pl.ds(0, PIV)], fp.at[pl.ds(own, 32), :], local.at[0])
    fj_own = pltpu.make_async_copy(feat, fj.at[pl.ds(own, 32), :], local.at[1])
    dp_own = pltpu.make_async_copy(damp, dp, local.at[2])

    def dcopy(k):
        return rcopy(damp, dp, d_send.at[k], d_recv, (lax.rem(w + k, 32), z))

    @pl.when(z == 0)
    def _():
        for k in (4, 3, 5, 2, 6, 1, 7):
            fpz(k).start()
        fp_own.start()

    @pl.when(w == 0)
    def _():
        @pl.loop(1, 32)
        def _(k):
            dcopy(k).start()

        dp_own.start()

    fj_own.start()

    sends = []

    def send_block(da, db, half, to, as_da, as_db, src=None):
        n = len(sends)
        r = row(da, db, c)
        if half is None:
            rows, index = pl.ds(r, 32), (as_da * 4 + as_db) * 2
        else:
            rows, index = pl.ds(r + 16 * half, 16), (as_da * 4 + as_db) * 2 + half
        op = rcopy(
            fj.at[rows, :] if src is None else src, fj.at[rows, :],
            ag_send.at[n], ag_recv.at[index], to,
        )
        op.start()
        sends.append(op)

    def wait_block(da, db):
        r = row(da, db, c)
        base = (da * 4 + db) * 2
        if da == 2 and db == 0 or db == 2:
            for h in range(2):
                ref = fj.at[pl.ds(r + 16 * h, 16), :]
                rcopy(ref, ref, ag_send.at[0], ag_recv.at[base + h], partner).wait_recv()
        else:
            ref = fj.at[pl.ds(r, 32), :]
            rcopy(ref, ref, ag_send.at[0], ag_recv.at[base], partner).wait_recv()

    def to_partner(p):
        da, db = ORDER[p]
        ref = fj.at[pl.ds(row(da, db, c), 32), :]
        op = rcopy(feat if p == 0 else ref, ref, pt_send.at[p], pt_recv.at[p], partner)
        op.start()
        sends.append(op)

    def plane_event(p):
        da, db = ORDER[p]
        src = feat if p == 0 else None
        if p:
            wait_block(da, db)
        if db == 0:
            if da == 0:
                send_block(0, 0, None, dev(1, 0), 3, 0, src)
                send_block(0, 0, None, dev(3, 0), 1, 0, src)
            elif da == 3:
                send_block(3, 0, 0, dev(1, 0), 2, 0)
            elif da == 1:
                send_block(1, 0, 1, dev(3, 0), 2, 0)
            send_block(da, 0, None, dev(0, 1), da, 3, src)
            send_block(da, 0, None, dev(0, 3), da, 1, src)
        elif db == 3:
            send_block(da, 3, 0, dev(0, 1), da, 2)
        elif db == 1:
            send_block(da, 1, 1, dev(0, 3), da, 2)
        to_partner(p)

    def fp_direct(k):
        da, db = lax.div(k, 4), lax.rem(k, 4)
        back = lax.rem(4 - da, 4) * 4 + lax.rem(4 - db, 4)
        ref = fp.at[pl.ds(own, 32), :]
        return rcopy(ref, ref, fp_send.at[k], fp_recv.at[back], dev(da, db))

    half_rows = fp.at[pl.ds(pl.multiple_of(c * 512, 512), 512), :]
    fp_half = rcopy(half_rows, half_rows, fpp_send, fpp_recv, partner)

    def panel_start():
        @pl.when(z == 0)
        def _():
            fp_own.wait()

        @pl.when(z != 0)
        def _():
            fpz(0).wait_recv()

        @pl.loop(1, 16)
        def _(k):
            fp_direct(k).start()

    def panel_to_partner():
        @pl.loop(1, 16)
        def _(k):
            fp_direct(k).wait_recv()

        fp_half.start()

    home = lax.div(w, 4)
    d = lax.rem(z - home + 8, 8)
    sub = pl.multiple_of(lax.rem(w, 4) * 512, 512)
    up = (w, lax.rem(z + 1, 8))
    down = (w, lax.rem(z + 7, 8))
    hops_up = d
    hops_down = lax.rem(8 - d, 8)
    near = jnp.minimum(hops_up, hops_down)

    def z_rows(p, s):
        da = _table([o[0] for o in ORDER], p)
        db = _table([o[1] for o in ORDER], p)
        core = c if s == 0 else 1 - c
        return row(da, db, core)

    def z_copy(p, s, from_root, to, way):
        r = z_rows(p, s)
        dst = fi.at[pl.ds(r, 32), :]
        src = fj.at[pl.ds(r, 32), pl.ds(sub, 512)] if from_root else dst
        q = p * 2 + s
        return rcopy(src, dst, z_send.at[q * 2 + way], z_recv.at[q], to)

    def pt_wait(p):
        ref = fj.at[pl.ds(z_rows(p, 1), 32), :]
        rcopy(ref, ref, pt_send.at[0], pt_recv.at[p], partner).wait_recv()

    def z_step(t):
        first = t - 1

        @pl.when((d == 0) & (first >= 0) & (first < RELAYED))
        def _():
            z_copy(first, 0, True, up, 0).start()
            pt_wait(first)
            z_copy(first, 1, True, down, 1).start()

        @pl.when((d == 0) & (first >= RELAYED) & (first < 16))
        def _():
            z_copy(first, 0, True, up, 0).start()
            z_copy(first, 0, True, down, 1).start()
            pt_wait(first)
            z_copy(first, 1, True, up, 0).start()
            z_copy(first, 1, True, down, 1).start()

        pu = first - 2 * hops_up

        @pl.when((d != 0) & (pu >= 0) & (pu < RELAYED))
        def _():
            z_copy(pu, 0, False, up, 0).wait_recv()

            @pl.when(d < 7)
            def _():
                z_copy(pu, 0, False, up, 0).start()

        pd = first - 2 * hops_down

        @pl.when((d != 0) & (pd >= 0) & (pd < RELAYED))
        def _():
            z_copy(pd, 1, False, down, 1).wait_recv()

            @pl.when(d > 1)
            def _():
                z_copy(pd, 1, False, down, 1).start()

        pn = first - 2 * near

        @pl.when((d != 0) & (pn >= RELAYED) & (pn < 16))
        def _():
            for s in range(2):
                z_copy(pn, s, False, up, 0).wait_recv()

                @pl.when(d < 4)
                def _():
                    z_copy(pn, s, False, up, 0).start()

                @pl.when(d > 5)
                def _():
                    z_copy(pn, s, False, down, 1).start()

    fj_wait = []
    for t in range(16):
        plane_event(t)
        if t == 0:
            fj_own.wait()
        if t == 4:
            panel_start()
        if t == 9:
            panel_to_partner()
        z_step(jnp.int32(t))
    z_step(jnp.int32(16))

    @pl.when(d != 0)
    def _():
        @pl.loop(0, 16)
        def _(p):
            pt_wait(p)

    fi_own = pltpu.make_async_copy(fj.at[:, pl.ds(sub, 512)], fi, local.at[3])

    @pl.when(d == 0)
    def _():
        fi_own.start()

    def scores_for(k):
        yk = lax.div(k, 2)
        xk = lax.rem(k, 2) * 2
        pieces = []
        for dx in range(2):
            for core in range(2):
                r = pl.multiple_of((core * 16 + yk * 4 + xk + dx) * 32, 32)
                pieces.append(fj[pl.ds(r, 32), :])
        return lax.dot_general(
            qry[...], jnp.concatenate(pieces, axis=0), (((1,), (1,)), ((), ())),
            preferred_element_type=F32,
        )

    def rs_copy(k):
        to = lax.rem(z + k, 8)
        return rcopy(part.at[to], inbox.at[k], rs_send.at[k], rs_recv.at[k], (w, to))

    @pl.loop(1, 8)
    def _(k):
        part[lax.rem(z + k, 8)] = scores_for(lax.rem(z + k, 8))
        rs_copy(k).start()

    part[z] = scores_for(z)

    @pl.loop(17, LAST_STEP)
    def _(t):
        z_step(t)

    total = part[z]
    for k in range(1, 8):
        rs_copy(k).wait_recv()
        total = total + inbox[k]
    sc[...] = total * (1.0 / math.sqrt(P_SIZE))

    @pl.when(d == 0)
    def _():
        fi_own.wait()

    fp_half.wait_recv()
    fp_half.wait_send()

    @pl.when(w == 0)
    def _():
        dp_own.wait()

        @pl.loop(1, 32)
        def _(k):
            dcopy(k).wait_send()

    @pl.when(w != 0)
    def _():
        dcopy(0).wait_recv()

    @pl.when(z == 0)
    def _():
        for k in range(1, 8):
            fpz(k).wait_send()

    @pl.loop(1, 16)
    def _(k):
        fp_direct(k).wait_send()

    @pl.loop(1, 8)
    def _(k):
        rs_copy(k).wait_send()

    for op in sends:
        op.wait_send()

    @pl.loop(0, 16)
    def _(p):
        one_way = p < RELAYED

        @pl.when(one_way & (d < 7))
        def _():
            z_copy(p, 0, False, up, 0).wait_send()

        @pl.when(one_way & (d != 1))
        def _():
            z_copy(p, 1, False, down, 1).wait_send()

        for s in range(2):
            @pl.when(jnp.logical_not(one_way) & (d < 4))
            def _():
                z_copy(p, s, False, up, 0).wait_send()

            @pl.when(jnp.logical_not(one_way) & ((d > 5) | (d == 0)))
            def _():
                z_copy(p, s, False, down, 1).wait_send()


def gather(features, queries, damping):
    vmem = pl.BlockSpec(memory_space=pltpu.VMEM)
    dma = pltpu.SemaphoreType.DMA
    return pl.pallas_call(
        gather_kernel,
        name="gather",
        out_shape=[
            jax.ShapeDtypeStruct((SLAB, 2048), BF16),
            jax.ShapeDtypeStruct((SLAB, 512), BF16),
            jax.ShapeDtypeStruct((SLAB, PIV), BF16),
            jax.ShapeDtypeStruct((4, 128), F32),
            jax.ShapeDtypeStruct((64, 128), F32),
        ],
        in_specs=[vmem] * 3,
        out_specs=[vmem] * 5,
        scratch_shapes=[
            pltpu.VMEM((8, 64, 128), F32),
            pltpu.VMEM((8, 64, 128), F32),
            dma((32,)), dma((40,)), dma((16,)), dma((16,)), dma((32,)), dma((64,)), dma(()), dma((8,)),
            dma((16,)), dma((16,)), dma(()), dma(()), dma(()), dma((32,)), dma((8,)), dma((8,)), dma((4,)),
        ],
        compiler_params=pltpu.CompilerParams(
            collective_id=0, has_side_effects=True, vmem_limit_bytes=32 * 1024 * 1024
        ),
    )(features, queries, damping)


def split2(v):
    hi = v.astype(BF16)
    return hi, (v - hi.astype(F32)).astype(BF16)


def split3(v):
    hi = v.astype(BF16)
    rest = v - hi.astype(F32)
    mid = rest.astype(BF16)
    return hi, mid, (rest - mid.astype(F32)).astype(BF16)


def tn(a, b):
    return lax.dot_general(a, b, (((0,), (0,)), ((), ())), preferred_element_type=F32)


def nn(a, b):
    return lax.dot_general(a, b, (((1,), (0,)), ((), ())), preferred_element_type=F32)


def nt(a, b):
    return lax.dot_general(a, b, (((1,), (1,)), ((), ())), preferred_element_type=F32)


WIDTH = 32


def factor_kernel(fp, dp, out, mat):
    rows = lax.broadcasted_iota(jnp.int32, (PIV, PIV), 0)
    cols = lax.broadcasted_iota(jnp.int32, (PIV, PIV), 1)
    diag = jnp.concatenate([dp[0:1, :], dp[1:2, :]], axis=1)
    mat[...] = tn(fp[...], fp[...]) * (1.0 / SLAB) + jnp.where(rows == cols, diag, 0.0)

    row_w = lax.broadcasted_iota(jnp.int32, (WIDTH, 1), 0)
    lane_w = lax.broadcasted_iota(jnp.int32, (WIDTH, PIV), 1)
    aug_eye = jnp.where(
        lax.broadcasted_iota(jnp.int32, (WIDTH, 128), 0) == lax.broadcasted_iota(jnp.int32, (WIDTH, 128), 1),
        jnp.float32(1.0), jnp.float32(0.0),
    )

    @pl.loop(0, PIV // WIDTH)
    def _(k):
        c0 = pl.multiple_of(k * WIDTH, WIDTH)
        r = pltpu.roll(mat[pl.ds(c0, WIDTH), :], lax.rem(PIV - c0, PIV), 1)
        aug = aug_eye
        scale = jnp.zeros((WIDTH, 1), F32)
        for j0 in range(0, WIDTH, 8):
            column = [jnp.broadcast_to(r[:, j0 + t : j0 + t + 1], (WIDTH, 128)) for t in range(8)]
            for t in range(8):
                j = j0 + t
                pivot = column[t][j : j + 1, :]
                scale = scale + jnp.where(row_w == j, pivot[:, 0:1], 0.0)
                m = jnp.where(row_w > j, column[t] * (1.0 / pivot), 0.0)
                for u in range(t + 1, 8):
                    column[u] = column[u] - m * column[u][j : j + 1, :]
                r = r - jnp.concatenate([m, m], axis=1) * r[j : j + 1, :]
                aug = aug - m * aug[j : j + 1, :]
        s = lax.rsqrt(scale)
        s = s * (1.5 - 0.5 * scale * s * s)
        r = r * s
        aug = aug * s
        r = pltpu.roll(r, c0, 1)
        aug = pltpu.roll(jnp.concatenate([aug, jnp.zeros((WIDTH, 128), F32)], axis=1), c0, 1)
        inside = (lane_w >= c0) & (lane_w < c0 + WIDTH)
        v = jnp.where(inside, aug, r)
        mat[pl.ds(c0, WIDTH), :] = v
        below = jnp.where(lane_w >= c0 + WIDTH, r, 0.0)
        a1, a2, a3 = split3(below)
        b1, b2, b3 = split3(v)
        lhs = jnp.concatenate([a1, a1, a2, a1, a2, a3], axis=0)
        rhs = jnp.concatenate([b1, b2, b1, b3, b2, b1], axis=0)
        change = tn(lhs, rhs)
        old = mat[...]
        fresh = (cols >= c0) & (cols < c0 + WIDTH) & (rows >= c0 + WIDTH)
        mat[...] = jnp.where(fresh, 0.0, old) - change

    out[...] = jnp.where(rows >= cols, mat[...], 0.0)


def factor_inverse(fp, dp):
    vmem = pl.BlockSpec(memory_space=pltpu.VMEM)
    return pl.pallas_call(
        factor_kernel,
        name="factor",
        out_shape=jax.ShapeDtypeStruct((PIV, PIV), F32),
        in_specs=[vmem] * 2,
        out_specs=vmem,
        scratch_shapes=[pltpu.VMEM((PIV, PIV), F32)],
    )(fp, dp)


TILE = 512


def final_kernel(fj, fi, fp, linv, drow, sc, kout, fout, sout, fit, fpt, xcat, lcat):
    w = lax.axis_index("wide")
    z = lax.axis_index("narrow")
    t = pl.program_id(0)

    @pl.when(t == 0)
    def _():
        fit[...] = (fi[...] * jnp.asarray(1.0 / SLAB, BF16)).T
        fpt[...] = (fp[...] * jnp.asarray(1.0 / SLAB, BF16)).T
        l1, l2, l3 = split3(linv[...])
        lcat[:, 0:256] = l1
        lcat[:, 256:512] = l2
        lcat[:, 512:768] = l3
        a = nn(fit[...], fp[...])
        row = w * 512 + lax.broadcasted_iota(jnp.int32, (512, PIV), 0)
        col = lax.broadcasted_iota(jnp.int32, (512, PIV), 1)
        damp = jnp.broadcast_to(drow[...], (512, PIV))
        a = a + jnp.where(row == col, damp, 0.0)
        a1, a2, a3 = split3(a)
        xrow = (
            nt(a1, l1) + (nt(a1, l2) + nt(a2, l1)) + (nt(a1, l3) + nt(a2, l2) + nt(a3, l1))
        )
        xrow = jnp.where((row < 128) & (col >= 128), 0.0, xrow)
        fout[...] = xrow
        hi, lo = split2(xrow)
        xcat[:, 0:256] = -hi
        xcat[:, 256:512] = -hi
        xcat[:, 512:768] = -lo
        sout[...] = sc[...]

    b = nn(fpt[...], fj[...])
    b1, b2, b3 = split3(b)
    l1, l2, l3 = lcat[:, 0:256], lcat[:, 256:512], lcat[:, 512:768]
    xt = nn(l1, b1) + (nn(l1, b2) + nn(l2, b1))
    hi, lo = split2(xt)
    k = nn(fit[...], fj[...]) + nn(xcat[...], jnp.concatenate([hi, lo, hi], axis=0))
    row = w * 512 + lax.broadcasted_iota(jnp.int32, (512, TILE), 0)
    col = z * 2048 + t * TILE + lax.broadcasted_iota(jnp.int32, (512, TILE), 1)
    damp = jnp.broadcast_to(drow[...], (512, TILE))
    k = k + jnp.where(row == col, damp, 0.0)
    kout[...] = jnp.where((row < PIV) | (col < PIV), 0.0, k)


def finish(fj, fi, fp, linv, drow, sc):
    def whole(shape):
        return pl.BlockSpec(shape, lambda t: (0,) * len(shape))

    return pl.pallas_call(
        final_kernel,
        name="finish",
        grid=(2048 // TILE,),
        out_shape=[
            jax.ShapeDtypeStruct((512, 2048), F32),
            jax.ShapeDtypeStruct((512, PIV), F32),
            jax.ShapeDtypeStruct((64, 128), F32),
        ],
        in_specs=[
            pl.BlockSpec((SLAB, TILE), lambda t: (0, t)),
            whole((SLAB, 512)), whole((SLAB, PIV)), whole((PIV, PIV)), whole((512, 1)), whole((64, 128)),
        ],
        out_specs=[pl.BlockSpec((512, TILE), lambda t: (0, t)), whole((512, PIV)), whole((64, 128))],
        scratch_shapes=[
            pltpu.VMEM((512, SLAB), BF16),
            pltpu.VMEM((PIV, SLAB), BF16),
            pltpu.VMEM((512, 768), BF16),
            pltpu.VMEM((PIV, 768), BF16),
        ],
        compiler_params=pltpu.CompilerParams(vmem_limit_bytes=40 * 1024 * 1024),
    )(fj, fi, fp, linv, drow, sc)


def on_device(features, queries, damping):
    fj, fi, fp, dp, sc = gather(features, queries, damping.reshape(4, 128))
    linv = factor_inverse(fp, dp)
    return tuple(finish(fj, fi, fp, linv, damping.reshape(512, 1), sc))


def solution(mesh):
    return jax.shard_map(
        on_device,
        mesh=mesh,
        in_specs=(P("wide", "narrow"), P("wide", "narrow"), P("wide")),
        out_specs=(P("wide", "narrow"), P("wide", None), P("wide", "narrow")),
        check_vma=False,
    )
```

time: 484 us -> 90.1 us (0.19)
  the two profiles are of different devices: /device:TPU:1 before, /device:TPU:16 now
where the time goes in v1:
time: 90.1 us; the launch traced here: 89.8 us
  Pallas kernels  78.2 us (87%)
  local copies, waits for them, and re-layouts  10.9 us (12%)
    pallas_call x1, Pallas kernels, gather(): pl.pallas_call(gather_kernel, name='gather', out_shape=[jax.ShapeDtypeStr...  55.8 us
    pallas_call x1, Pallas kernels, factor_inverse(): pl.pallas_call(factor_kernel, name='factor', out_shape=jax.ShapeDtypeStru...  11.9 us
    pallas_call x1, Pallas kernels, finish(): pl.pallas_call(final_kernel, name='finish', grid=(2048 // TILE,), out_sha...  10.5 us
    unnamed x18, local copies, waits for them, and re-layouts  10.1 us

profile of v1, /device:TPU:16, one launch (start us, length us, event | category | flops | bytes accessed | tf_op | source)
XLA Modules:
  0.0 89.8 jit_solution(13897400406524042591)
XLA Ops:
  0.6 0.8 copy.6.drow
  1.5 0.0 copy-start.5
  1.5 0.9 %copy-done.5 = bf16[64,2048]{1,0:T(8,128)(2,1)S(1)} copy-done((bf16[64,2048]{1,0:T(8,128)(2,1)S(1)}, bf16[64,2048]{1,0:T(8,128)(2,1)}, u32[]{:S(2)}) %copy-start.5) | copy-done | bytes 262168
  2.4 0.0 copy-start.6
  2.4 0.9 %copy-done.6 = bf16[32,2048]{1,0:T(8,128)(2,1)S(1)} copy-done((bf16[32,2048]{1,0:T(8,128)(2,1)S(1)}, bf16[32,2048]{1,0:T(8,128)(2,1)}, u32[]{:S(2)}) %copy-start.6) | copy-done | bytes 131096
  3.3 0.0 copy-start.7
  3.3 0.7 copy-done.7
  4.0 55.8 %gather.1 = (bf16[1024,2048]{1,0:T(8,128)(2,1)S(1)}, bf16[1024,512]{1,0:T(8,128)(2,1)S(1)}, bf16[1024,256]{1,0:T(8,128)(2,1)S(1)}, f32[4,128]{1,0:T(4,128)S(1)}, f32[64,128]{1,0:T(8,128)S(1)}) custom-call(bf16[32,2048]{1,0:T(8,128)(2,1)S(1)} %copy-done.6, bf16[64,2048]{1,0:T(8,128)(2,1)S(1)} %copy-done.5, f32[4,128]{1,0:T(4,128)S(1)} %bitcast.3), custom_call_target="tpu_custom_call" | custom-call | tf_op jit(solution)/shard_map/gather/pallas_call | solution.py:388
  59.8 0.0 copy-start
  59.8 2.0 %copy-done = bf16[1024,2048]{1,0:T(8,128)(2,1)} copy-done((bf16[1024,2048]{1,0:T(8,128)(2,1)}, bf16[1024,2048]{1,0:T(8,128)(2,1)S(1)}, u32[]{:S(2)}) %copy-start) | copy-done | bytes 4194328
  61.8 0.0 copy-start.2
  61.8 0.8 copy-done.2
  62.6 0.0 copy-start.8
  62.6 0.6 copy-done.8
  63.2 11.9 %factor.1.linv = f32[256,256]{1,0:T(8,128)} custom-call(bf16[1024,256]{1,0:T(8,128)(2,1)} %copy-done.2, f32[4,128]{1,0:T(4,128)} %copy-done.8), custom_call_target="tpu_custom_call" | custom-call | tf_op jit(solution)/shard_map/factor/pallas_call | solution.py:493
  75.1 0.0 copy-start.1
  75.1 2.2 %copy-done.1 = bf16[1024,2048]{1,0:T(8,128)(2,1)S(1)} copy-done((bf16[1024,2048]{1,0:T(8,128)(2,1)S(1)}, bf16[1024,2048]{1,0:T(8,128)(2,1)}, u32[]{:S(2)}) %copy-start.1) | copy-done | bytes 4194328
  77.3 0.0 copy-start.3
  77.3 1.0 %copy-done.3 = bf16[1024,256]{1,0:T(8,128)(2,1)S(1)} copy-done((bf16[1024,256]{1,0:T(8,128)(2,1)S(1)}, bf16[1024,256]{1,0:T(8,128)(2,1)}, u32[]{:S(2)}) %copy-start.3) | copy-done | bytes 524312
  78.3 0.0 copy-start.4
  78.3 0.9 %copy-done.4 = f32[256,256]{1,0:T(8,128)S(1)} copy-done((f32[256,256]{1,0:T(8,128)S(1)}, f32[256,256]{1,0:T(8,128)}, u32[]{:S(2)}) %copy-start.4) | copy-done | bytes 262168
  79.3 10.5 %finish.1 = (f32[512,2048]{1,0:T(8,128)}, f32[512,256]{1,0:T(8,128)}, f32[64,128]{1,0:T(8,128)}) custom-call(bf16[1024,2048]{1,0:T(8,128)(2,1)S(1)} %copy-done.1, bf16[1024,512]{1,0:T(8,128)(2,1)S(1)} %get-tuple-element.9.fi, bf16[1024,256]{1,0:T(8,128)(2,1)S(1)} %copy-done.3, f32[256,256]{1,0:T(8,128)S(1)} %copy-done.4, f32[512,1]{1,0:T(8,128)S(1)} %copy.6.drow, ...), custom_call_target="tpu_custom_call" | custom-call | tf_op jit(solution)/shard_map/finish/pallas_call | solution.py:553
Async XLA Ops:
  1.5 1.0 %copy-start.5 = (bf16[64,2048]{1,0:T(8,128)(2,1)S(1)}, bf16[64,2048]{1,0:T(8,128)(2,1)}, u32[]{:S(2)}) copy-start(bf16[64,2048]{1,0:T(8,128)(2,1)} %qry.1) | copy-start | bytes 786436
  2.4 0.9 %copy-start.6 = (bf16[32,2048]{1,0:T(8,128)(2,1)S(1)}, bf16[32,2048]{1,0:T(8,128)(2,1)}, u32[]{:S(2)}) copy-start(bf16[32,2048]{1,0:T(8,128)(2,1)} %feat.1) | copy-start | bytes 393220
  3.3 0.7 copy-start.7
  59.8 2.0 %copy-start = (bf16[1024,2048]{1,0:T(8,128)(2,1)}, bf16[1024,2048]{1,0:T(8,128)(2,1)S(1)}, u32[]{:S(2)}) copy-start(bf16[1024,2048]{1,0:T(8,128)(2,1)S(1)} %get-tuple-element.8.fj) | copy-start | bytes 12582916
  61.8 0.8 copy-start.2
  62.6 0.6 copy-start.8
  75.1 2.2 %copy-start.1 = (bf16[1024,2048]{1,0:T(8,128)(2,1)S(1)}, bf16[1024,2048]{1,0:T(8,128)(2,1)}, u32[]{:S(2)}) copy-start(bf16[1024,2048]{1,0:T(8,128)(2,1)} %copy-done) | copy-start | bytes 12582916
  77.3 1.0 %copy-start.3 = (bf16[1024,256]{1,0:T(8,128)(2,1)S(1)}, bf16[1024,256]{1,0:T(8,128)(2,1)}, u32[]{:S(2)}) copy-start(bf16[1024,256]{1,0:T(8,128)(2,1)} %copy-done.2) | copy-start | bytes 1572868
  78.3 0.9 %copy-start.4 = (f32[256,256]{1,0:T(8,128)S(1)}, f32[256,256]{1,0:T(8,128)}, u32[]{:S(2)}) copy-start(f32[256,256]{1,0:T(8,128)} %factor.1.linv) | copy-start | bytes 786436

commit v2 on v1

v2 whole, which is shorter than its diff:
```python
import functools
import math

import jax
import jax.numpy as jnp
from jax import lax
from jax.experimental import pallas as pl
from jax.experimental.pallas import tpu as pltpu
from jax.sharding import PartitionSpec as P

P_SIZE = 16384
PIV = 256
SLAB = 1024
MESH = pl.DeviceIdType.MESH
F32 = jnp.float32
BF16 = jnp.bfloat16

ORDER = (
    (0, 0), (3, 0), (1, 0), (0, 3), (0, 1), (2, 0), (3, 3), (1, 3),
    (3, 1), (1, 1), (2, 3), (2, 1), (0, 2), (3, 2), (1, 2), (2, 2),
)
RELAYED = 10
LAST_STEP = 25


def _table(values, p):
    out = jnp.int32(0)
    for k, v in enumerate(values):
        if v:
            out = out + jnp.where(p == k, jnp.int32(v), jnp.int32(0))
    return out


def split2(v):
    hi = v.astype(BF16)
    return hi, (v - hi.astype(F32)).astype(BF16)


def split3(v):
    hi = v.astype(BF16)
    rest = v - hi.astype(F32)
    mid = rest.astype(BF16)
    return hi, mid, (rest - mid.astype(F32)).astype(BF16)


def tn(a, b):
    return lax.dot_general(a, b, (((0,), (0,)), ((), ())), preferred_element_type=F32)


def nn(a, b):
    return lax.dot_general(a, b, (((1,), (0,)), ((), ())), preferred_element_type=F32)


def nt(a, b):
    return lax.dot_general(a, b, (((1,), (1,)), ((), ())), preferred_element_type=F32)


WIDTH = 32
PANELS = PIV // WIDTH
TILE = 512


def panel_step(k, mat, rows, cols):
    row_w = lax.broadcasted_iota(jnp.int32, (WIDTH, 1), 0)
    lane_w = lax.broadcasted_iota(jnp.int32, (WIDTH, PIV), 1)
    aug = jnp.where(
        lax.broadcasted_iota(jnp.int32, (WIDTH, 128), 0) == lax.broadcasted_iota(jnp.int32, (WIDTH, 128), 1),
        jnp.float32(1.0), jnp.float32(0.0),
    )
    c0 = pl.multiple_of(k * WIDTH, WIDTH)
    r = pltpu.roll(mat[pl.ds(c0, WIDTH), :], lax.rem(PIV - c0, PIV), 1)
    scale = jnp.zeros((WIDTH, 1), F32)
    for j0 in range(0, WIDTH, 8):
        column = [jnp.broadcast_to(r[:, j0 + t : j0 + t + 1], (WIDTH, 128)) for t in range(8)]
        for t in range(8):
            j = j0 + t
            pivot = column[t][j : j + 1, :]
            scale = scale + jnp.where(row_w == j, pivot[:, 0:1], 0.0)
            m = jnp.where(row_w > j, column[t] * (1.0 / pivot), 0.0)
            for u in range(t + 1, 8):
                column[u] = column[u] - m * column[u][j : j + 1, :]
            r = r - jnp.concatenate([m, m], axis=1) * r[j : j + 1, :]
            aug = aug - m * aug[j : j + 1, :]
    s = lax.rsqrt(scale)
    s = s * (1.5 - 0.5 * scale * s * s)
    r = r * s
    aug = aug * s
    r = pltpu.roll(r, c0, 1)
    aug = pltpu.roll(jnp.concatenate([aug, jnp.zeros((WIDTH, 128), F32)], axis=1), c0, 1)
    inside = (lane_w >= c0) & (lane_w < c0 + WIDTH)
    v = jnp.where(inside, aug, r)
    mat[pl.ds(c0, WIDTH), :] = v
    below = jnp.where(lane_w >= c0 + WIDTH, r, 0.0)
    a1, a2, a3 = split3(below)
    b1, b2, b3 = split3(v)
    lhs = jnp.concatenate([a1, a1, a2, a1, a2, a3], axis=0)
    rhs = jnp.concatenate([b1, b2, b1, b3, b2, b1], axis=0)
    change = tn(lhs, rhs)
    fresh = (cols >= c0) & (cols < c0 + WIDTH) & (rows >= c0 + WIDTH)
    mat[...] = jnp.where(fresh, 0.0, mat[...]) - change


def gather_kernel(
    feat, qry_hbm, damp, fj, fi, fp, linv, xhi, xlo, sc,
    qry, dp, fpt, mat, part, inbox,
    ag_recv, ag_send, pt_recv, pt_send, z_recv, z_send, fpz_recv, fpz_send,
    fp_recv, fp_send, fpp_recv, fpp_send, d_recv, d_send, rs_recv, rs_send, local,
):
    w = lax.axis_index("wide")
    z = lax.axis_index("narrow")
    c = lax.rem(w, 2)
    x = lax.rem(lax.div(w, 2), 4)
    y = lax.div(w, 8)

    def spot(da, db, core):
        px = lax.rem(x + da + core * (db - da), 4)
        py = lax.rem(y + db + core * (da - db), 4)
        return px, py

    def dev(da, db):
        px, py = spot(da, db, c)
        return ((py * 4 + px) * 2 + c, z)

    def row(da, db, core):
        px, py = spot(da, db, core)
        return pl.multiple_of((core * 16 + py * 4 + px) * 32, 32)

    partner = (w + 1 - 2 * c, z)
    own = row(0, 0, c)

    def rcopy(src, dst, ssem, rsem, to):
        return pltpu.make_async_remote_copy(
            src_ref=src, dst_ref=dst, send_sem=ssem, recv_sem=rsem, device_id=to, device_id_type=MESH
        )

    fj_own = pltpu.make_async_copy(feat, fj.at[pl.ds(own, 32), :], local.at[1])
    fj_own.start()
    qry_copy = pltpu.make_async_copy(qry_hbm, qry, local.at[2])
    qry_copy.start()
    dp_own = pltpu.make_async_copy(damp, dp, local.at[4])

    @pl.when(w == 0)
    def _():
        dp_own.start()

    barrier = pltpu.get_barrier_semaphore()

    @pl.loop(1, 16)
    def _(k):
        pl.semaphore_signal(
            barrier, inc=1, device_id=dev(lax.div(k, 4), lax.rem(k, 4)), device_id_type=MESH
        )

    @pl.loop(1, 8)
    def _(k):
        pl.semaphore_signal(barrier, inc=1, device_id=(w, lax.rem(z + k, 8)), device_id_type=MESH)

    pl.semaphore_signal(barrier, inc=1, device_id=partner, device_id_type=MESH)
    fj_own.wait()
    pl.semaphore_wait(barrier, 23)

    def fpz(k):
        return rcopy(
            fj.at[pl.ds(own, 32), pl.ds(0, PIV)], fp.at[pl.ds(own, 32), :], fpz_send.at[k], fpz_recv,
            (w, lax.rem(z + k, 8)),
        )

    fp_own = pltpu.make_async_copy(
        fj.at[pl.ds(own, 32), pl.ds(0, PIV)], fp.at[pl.ds(own, 32), :], local.at[0]
    )

    def dcopy(k):
        return rcopy(dp, dp, d_send.at[k], d_recv, dev(lax.div(k, 4), lax.rem(k, 4)))

    d_across = rcopy(dp, dp, d_send.at[16], d_recv, partner)

    @pl.when(z == 0)
    def _():
        for k in (4, 3, 5, 2, 6, 1, 7):
            fpz(k).start()
        fp_own.start()

    @pl.when(w == 0)
    def _():
        dp_own.wait()

        @pl.loop(1, 16)
        def _(k):
            dcopy(k).start()


    sends = []

    def send_block(da, db, half, to, as_da, as_db):
        n = len(sends)
        r = row(da, db, c)
        if half is None:
            rows, index = pl.ds(r, 32), (as_da * 4 + as_db) * 2
        else:
            rows, index = pl.ds(r + 16 * half, 16), (as_da * 4 + as_db) * 2 + half
        op = rcopy(
            fj.at[rows, :], fj.at[rows, :],
            ag_send.at[n], ag_recv.at[index], to,
        )
        op.start()
        sends.append(op)

    def wait_block(da, db):
        r = row(da, db, c)
        base = (da * 4 + db) * 2
        if da == 2 and db == 0 or db == 2:
            for h in range(2):
                ref = fj.at[pl.ds(r + 16 * h, 16), :]
                rcopy(ref, ref, ag_send.at[0], ag_recv.at[base + h], partner).wait_recv()
        else:
            ref = fj.at[pl.ds(r, 32), :]
            rcopy(ref, ref, ag_send.at[0], ag_recv.at[base], partner).wait_recv()

    def to_partner(p):
        da, db = ORDER[p]
        ref = fj.at[pl.ds(row(da, db, c), 32), :]
        op = rcopy(ref, ref, pt_send.at[p], pt_recv.at[p], partner)
        op.start()
        sends.append(op)

    def plane_event(p):
        da, db = ORDER[p]
        if p:
            wait_block(da, db)
        if db == 0:
            if da == 0:
                send_block(0, 0, None, dev(1, 0), 3, 0)
                send_block(0, 0, None, dev(3, 0), 1, 0)
            elif da == 3:
                send_block(3, 0, 0, dev(1, 0), 2, 0)
            elif da == 1:
                send_block(1, 0, 1, dev(3, 0), 2, 0)
            send_block(da, 0, None, dev(0, 1), da, 3)
            send_block(da, 0, None, dev(0, 3), da, 1)
        elif db == 3:
            send_block(da, 3, 0, dev(0, 1), da, 2)
        elif db == 1:
            send_block(da, 1, 1, dev(0, 3), da, 2)
        to_partner(p)

    def fp_direct(k):
        da, db = lax.div(k, 4), lax.rem(k, 4)
        back = lax.rem(4 - da, 4) * 4 + lax.rem(4 - db, 4)
        ref = fp.at[pl.ds(own, 32), :]
        return rcopy(ref, ref, fp_send.at[k], fp_recv.at[back], dev(da, db))

    half_rows = fp.at[pl.ds(pl.multiple_of(c * 512, 512), 512), :]
    fp_half = rcopy(half_rows, half_rows, fpp_send, fpp_recv, partner)

    def panel_start():
        @pl.when(z == 0)
        def _():
            fp_own.wait()

        @pl.when(z != 0)
        def _():
            fpz(0).wait_recv()

        @pl.loop(1, 16)
        def _(k):
            fp_direct(k).start()

    def panel_to_partner():
        @pl.loop(1, 16)
        def _(k):
            fp_direct(k).wait_recv()

        fp_half.start()

        @pl.when(c == 0)
        def _():
            @pl.when(w != 0)
            def _():
                dcopy(0).wait_recv()

            d_across.start()

    home = lax.div(w, 4)
    d = lax.rem(z - home + 8, 8)
    sub = pl.multiple_of(lax.rem(w, 4) * 512, 512)
    up = (w, lax.rem(z + 1, 8))
    down = (w, lax.rem(z + 7, 8))
    hops_up = d
    hops_down = lax.rem(8 - d, 8)
    near = jnp.minimum(hops_up, hops_down)

    def z_rows(p, s):
        da = _table([o[0] for o in ORDER], p)
        db = _table([o[1] for o in ORDER], p)
        core = c if s == 0 else 1 - c
        return row(da, db, core)

    def z_copy(p, s, from_root, to, way):
        r = z_rows(p, s)
        dst = fi.at[pl.ds(r, 32), :]
        src = fj.at[pl.ds(r, 32), pl.ds(sub, 512)] if from_root else dst
        q = p * 2 + s
        return rcopy(src, dst, z_send.at[q * 2 + way], z_recv.at[q], to)

    def pt_wait(p):
        ref = fj.at[pl.ds(z_rows(p, 1), 32), :]
        rcopy(ref, ref, pt_send.at[0], pt_recv.at[p], partner).wait_recv()

    def z_step(t):
        first = t - 1

        @pl.when((d == 0) & (first >= 0) & (first < RELAYED))
        def _():
            z_copy(first, 0, True, up, 0).start()
            pt_wait(first)
            z_copy(first, 1, True, down, 1).start()

        @pl.when((d == 0) & (first >= RELAYED) & (first < 16))
        def _():
            z_copy(first, 0, True, up, 0).start()
            z_copy(first, 0, True, down, 1).start()
            pt_wait(first)
            z_copy(first, 1, True, up, 0).start()
            z_copy(first, 1, True, down, 1).start()

        pu = first - 2 * hops_up

        @pl.when((d != 0) & (pu >= 0) & (pu < RELAYED))
        def _():
            z_copy(pu, 0, False, up, 0).wait_recv()

            @pl.when(d < 7)
            def _():
                z_copy(pu, 0, False, up, 0).start()

        pd = first - 2 * hops_down

        @pl.when((d != 0) & (pd >= 0) & (pd < RELAYED))
        def _():
            z_copy(pd, 1, False, down, 1).wait_recv()

            @pl.when(d > 1)
            def _():
                z_copy(pd, 1, False, down, 1).start()

        pn = first - 2 * near

        @pl.when((d != 0) & (pn >= RELAYED) & (pn < 16))
        def _():
            for s in range(2):
                z_copy(pn, s, False, up, 0).wait_recv()

                @pl.when(d < 4)
                def _():
                    z_copy(pn, s, False, up, 0).start()

                @pl.when(d > 5)
                def _():
                    z_copy(pn, s, False, down, 1).start()

    def plane_tail(p):
        r = z_rows(p, 0)
        da = _table([o[0] for o in ORDER], p)
        for h in range(2):
            ref = fj.at[pl.ds(r + 16 * h, 16), :]
            rcopy(ref, ref, ag_send.at[0], ag_recv.at[(da * 4 + 2) * 2 + h], partner).wait_recv()
        ref = fj.at[pl.ds(r, 32), :]
        rcopy(ref, ref, pt_send.at[p], pt_recv.at[p], partner).start()

    fi_own = pltpu.make_async_copy(fj.at[:, pl.ds(sub, 512)], fi, local.at[3])

    def scores_for(k):
        yk = lax.div(k, 2)
        xk = lax.rem(k, 2) * 2
        pieces = []
        for dx in range(2):
            for core in range(2):
                r = pl.multiple_of((core * 16 + yk * 4 + xk + dx) * 32, 32)
                pieces.append(fj[pl.ds(r, 32), :])
        return lax.dot_general(
            qry[...], jnp.concatenate(pieces, axis=0), (((1,), (1,)), ((), ())),
            preferred_element_type=F32,
        )

    def rs_copy(k):
        to = lax.rem(z + k, 8)
        return rcopy(part.at[to], inbox.at[k], rs_send.at[k], rs_recv.at[k], (w, to))

    def plane_done():
        @pl.when(d != 0)
        def _():
            @pl.loop(0, 16)
            def _(p):
                pt_wait(p)

        @pl.when(d == 0)
        def _():
            fi_own.start()

        qry_copy.wait()

        @pl.loop(1, 8)
        def _(k):
            part[lax.rem(z + k, 8)] = scores_for(lax.rem(z + k, 8))
            rs_copy(k).start()

        part[z] = scores_for(z)

    for t in range(12):
        plane_event(t)
        if t == 4:
            panel_start()
        if t == 9:
            panel_to_partner()
        z_step(jnp.int32(t))

    fp_half.wait_recv()

    @pl.when(c != 0)
    def _():
        d_across.wait_recv()

    rows = lax.broadcasted_iota(jnp.int32, (PIV, PIV), 0)
    cols = lax.broadcasted_iota(jnp.int32, (PIV, PIV), 1)
    diag = jnp.concatenate([dp[0:1, :], dp[1:2, :]], axis=1)
    fpt[...] = (fp[...] * jnp.asarray(1.0 / SLAB, BF16)).T
    mat[...] = nn(fpt[...], fp[...]) + jnp.where(rows == cols, diag, 0.0)

    @pl.loop(0, PANELS)
    def _(k):
        @pl.when(k < 4)
        def _():
            plane_tail(12 + k)

        z_step(12 + k)

        @pl.when(k == 4)
        def _():
            plane_done()

        panel_step(k, mat, rows, cols)

    linv[...] = jnp.where(rows >= cols, mat[...], 0.0)

    @pl.loop(0, 2048 // TILE)
    def _(t):
        z_step(12 + PANELS + t)
        lanes = pl.ds(pl.multiple_of(t * TILE, TILE), TILE)
        b1, b2, _b = split3(nn(fpt[...], fj[:, lanes]))
        l1, l2, _l = split3(linv[...])
        hi, lo = split2(nn(l1, b1) + (nn(l1, b2) + nn(l2, b1)))
        xhi[:, lanes] = hi
        xlo[:, lanes] = lo

    @pl.loop(12 + PANELS + 2048 // TILE, LAST_STEP)
    def _(t):
        z_step(t)

    total = part[z]
    for k in range(1, 8):
        rs_copy(k).wait_recv()
        total = total + inbox[k]
    sc[...] = total * (1.0 / math.sqrt(P_SIZE))

    @pl.when(d == 0)
    def _():
        fi_own.wait()

    fp_half.wait_send()

    @pl.when(w == 0)
    def _():
        @pl.loop(1, 16)
        def _(k):
            dcopy(k).wait_send()

    @pl.when(c == 0)
    def _():
        d_across.wait_send()

    @pl.when(z == 0)
    def _():
        for k in range(1, 8):
            fpz(k).wait_send()

    @pl.loop(1, 16)
    def _(k):
        fp_direct(k).wait_send()

    @pl.loop(1, 8)
    def _(k):
        rs_copy(k).wait_send()

    for op in sends:
        op.wait_send()

    @pl.loop(12, 16)
    def _(p):
        ref = fj.at[pl.ds(z_rows(p, 0), 32), :]
        rcopy(ref, ref, pt_send.at[p], pt_recv.at[p], partner).wait_send()

    @pl.loop(0, 16)
    def _(p):
        one_way = p < RELAYED

        @pl.when(one_way & (d < 7))
        def _():
            z_copy(p, 0, False, up, 0).wait_send()

        @pl.when(one_way & (d != 1))
        def _():
            z_copy(p, 1, False, down, 1).wait_send()

        for s in range(2):
            @pl.when(jnp.logical_not(one_way) & (d < 4))
            def _():
                z_copy(p, s, False, up, 0).wait_send()

            @pl.when(jnp.logical_not(one_way) & ((d > 5) | (d == 0)))
            def _():
                z_copy(p, s, False, down, 1).wait_send()


def gather(features, queries, damping):
    vmem = pl.BlockSpec(memory_space=pltpu.VMEM)
    hbm = pl.BlockSpec(memory_space=pltpu.HBM)
    dma = pltpu.SemaphoreType.DMA
    return pl.pallas_call(
        gather_kernel,
        name="gather",
        out_shape=[
            jax.ShapeDtypeStruct((SLAB, 2048), BF16),
            jax.ShapeDtypeStruct((SLAB, 512), BF16),
            jax.ShapeDtypeStruct((SLAB, PIV), BF16),
            jax.ShapeDtypeStruct((PIV, PIV), F32),
            jax.ShapeDtypeStruct((PIV, 2048), BF16),
            jax.ShapeDtypeStruct((PIV, 2048), BF16),
            jax.ShapeDtypeStruct((64, 128), F32),
        ],
        in_specs=[hbm] * 3,
        out_specs=[vmem] * 7,
        scratch_shapes=[
            pltpu.VMEM((64, 2048), BF16),
            pltpu.VMEM((4, 128), F32),
            pltpu.VMEM((PIV, SLAB), BF16),
            pltpu.VMEM((PIV, PIV), F32),
            pltpu.VMEM((8, 64, 128), F32),
            pltpu.VMEM((8, 64, 128), F32),
            dma((32,)), dma((40,)), dma((16,)), dma((16,)), dma((32,)), dma((64,)), dma(()), dma((8,)),
            dma((16,)), dma((16,)), dma(()), dma(()), dma(()), dma((17,)), dma((8,)), dma((8,)), dma((5,)),
        ],
        compiler_params=pltpu.CompilerParams(
            collective_id=0, has_side_effects=True, vmem_limit_bytes=40 * 1024 * 1024
        ),
    )(features, queries, damping)


def final_kernel(fj, xhi, xlo, fi, fp, linv, damp, sc, kout, fout, sout, fit, xcat):
    w = lax.axis_index("wide")
    z = lax.axis_index("narrow")
    t = pl.program_id(0)

    @pl.when(t == 0)
    def _():
        fit[...] = (fi[...] * jnp.asarray(1.0 / SLAB, BF16)).T
        a = nn(fit[...], fp[...])
        row = w * 512 + lax.broadcasted_iota(jnp.int32, (512, PIV), 0)
        col = lax.broadcasted_iota(jnp.int32, (512, PIV), 1)
        lanes = jnp.concatenate([damp[0:1, :], damp[1:2, :]], axis=1)
        a = a + jnp.where(row == col, lanes, 0.0)
        a1, a2, a3 = split3(a)
        l1, l2, l3 = split3(linv[...])
        xrow = (
            nt(a1, l1) + (nt(a1, l2) + nt(a2, l1)) + (nt(a1, l3) + nt(a2, l2) + nt(a3, l1))
        )
        xrow = jnp.where((row < 128) & (col >= 128), 0.0, xrow)
        fout[...] = xrow
        hi, lo = split2(xrow)
        xcat[:, 0:256] = -hi
        xcat[:, 256:512] = -hi
        xcat[:, 512:768] = -lo
        sout[...] = sc[...]

    k = nn(fit[...], fj[...]) + nn(xcat[...], jnp.concatenate([xhi[...], xlo[...], xhi[...]], axis=0))
    row = lax.broadcasted_iota(jnp.int32, (512, TILE), 0)
    lane = lax.broadcasted_iota(jnp.int32, (512, TILE), 1)
    col = z * 2048 + t * TILE
    lanes = jnp.concatenate([damp[i : i + 1, :] for i in range(4)], axis=1)
    k = k + jnp.where((row == lane) & (col == w * 512), lanes, 0.0)
    kout[...] = jnp.where((w * 512 + row < PIV) | (col + lane < PIV), 0.0, k)


def finish(fj, fi, fp, linv, xhi, xlo, sc, damping):
    def whole(shape):
        return pl.BlockSpec(shape, lambda t: (0,) * len(shape))

    def tiled(rows):
        return pl.BlockSpec((rows, TILE), lambda t: (0, t))

    return pl.pallas_call(
        final_kernel,
        name="finish",
        grid=(2048 // TILE,),
        out_shape=[
            jax.ShapeDtypeStruct((512, 2048), F32),
            jax.ShapeDtypeStruct((512, PIV), F32),
            jax.ShapeDtypeStruct((64, 128), F32),
        ],
        in_specs=[
            tiled(SLAB), tiled(PIV), tiled(PIV),
            whole((SLAB, 512)), whole((SLAB, PIV)), whole((PIV, PIV)), whole((4, 128)), whole((64, 128)),
        ],
        out_specs=[tiled(512), whole((512, PIV)), whole((64, 128))],
        scratch_shapes=[
            pltpu.VMEM((512, SLAB), BF16),
            pltpu.VMEM((512, 768), BF16),
        ],
        compiler_params=pltpu.CompilerParams(vmem_limit_bytes=40 * 1024 * 1024),
    )(fj, xhi, xlo, fi, fp, linv, damping, sc)


def on_device(features, queries, damping):
    damping = damping.reshape(4, 128)
    return tuple(finish(*gather(features, queries, damping), damping))


def solution(mesh):
    return jax.shard_map(
        on_device,
        mesh=mesh,
        in_specs=(P("wide", "narrow"), P("wide", "narrow"), P("wide")),
        out_specs=(P("wide", "narrow"), P("wide", None), P("wide", "narrow")),
        check_vma=False,
    )
```

time: 90.1 us -> 67.6 us (0.75)
  Pallas kernels: 78.2 us -> 64 us
  local copies, waits for them, and re-layouts: 10.9 us -> 2.53 us
    pallas_call x1 -> x0, Pallas kernels: 11.9 us -> none  [factor_inverse(): pl.pallas_call(factor_kernel, name='factor', out_shape=jax.ShapeDtypeStru...]
    unnamed x18 -> x6, local copies, waits for them, and re-layouts: 10.1 us -> 2.53 us
    pallas_call x1, Pallas kernels: 10.5 us -> 7.46 us  [finish(): pl.pallas_call(final_kernel, name='finish', grid=(2048 // TILE,), out_sha...]
where the time goes in v2:
time: 67.6 us; the launch traced here: 67.2 us
  Pallas kernels  64 us (95%)
  local copies, waits for them, and re-layouts  2.53 us (4%)
    pallas_call x1, Pallas kernels, gather(): pl.pallas_call(gather_kernel, name='gather', out_shape=[jax.ShapeDtypeStr...  56.5 us
    pallas_call x1, Pallas kernels, finish(): pl.pallas_call(final_kernel, name='finish', grid=(2048 // TILE,), out_sha...  7.46 us
    unnamed x6, local copies, waits for them, and re-layouts  2.53 us

profile of v2, /device:TPU:16, one launch (start us, length us, event | category | flops | bytes accessed | tf_op | source)
XLA Modules:
  0.0 67.2 jit_solution(17836131071042913794)
XLA Ops:
  0.6 0.0 copy-start
  0.6 0.9 %copy-done = bf16[64,2048]{1,0:T(8,128)(2,1)S(1)} copy-done((bf16[64,2048]{1,0:T(8,128)(2,1)S(1)}, bf16[64,2048]{1,0:T(8,128)(2,1)}, u32[]{:S(2)}) %copy-start) | copy-done | bytes 262168
  1.6 0.0 copy-start.1
  1.6 0.9 %copy-done.1 = bf16[32,2048]{1,0:T(8,128)(2,1)S(1)} copy-done((bf16[32,2048]{1,0:T(8,128)(2,1)S(1)}, bf16[32,2048]{1,0:T(8,128)(2,1)}, u32[]{:S(2)}) %copy-start.1) | copy-done | bytes 131096
  2.5 0.0 copy-start.2
  2.5 0.7 %copy-done.2 = f32[512]{0:T(512)S(1)} copy-done((f32[512]{0:T(512)S(1)}, f32[512]{0:T(512)}, u32[]{:S(2)}) %copy-start.2) | copy-done | bytes 2072
  3.2 56.5 %gather.1 = (bf16[1024,2048]{1,0:T(8,128)(2,1)S(1)}, bf16[1024,512]{1,0:T(8,128)(2,1)S(1)}, bf16[1024,256]{1,0:T(8,128)(2,1)S(1)}, f32[256,256]{1,0:T(8,128)S(1)...) custom-call(bf16[32,2048]{1,0:T(8,128)(2,1)S(1)} %copy-done.1, ...), custom_call_target="tpu_custom_call" | custom-call | tf_op jit(solution)/shard_map/gather/pallas_call | solution.py:528
  59.7 7.5 %finish.1 = (f32[512,2048]{1,0:T(8,128)}, f32[512,256]{1,0:T(8,128)}, f32[64,128]{1,0:T(8,128)}) custom-call(bf16[1024,2048]{1,0:T(8,128)(2,1)S(1)} %get-tuple-element.10.fj, bf16[256,2048]{1,0:T(8,128)(2,1)S(1)} %get-tuple-element.11.xhi, bf16[256,2048]{1,0:T(8,128)(2,1)S(1)} %get-tuple-element.12.xlo, bf16[1024,512]{1,0:T(8,128)(2,1)S(1)} %get-tuple-element.13.fi, ...), custom_call_target="tpu_custom_call" | custom-call | tf_op jit(solution)/shard_map/finish/pallas_call | solution.py:600
Async XLA Ops:
  0.6 1.0 %copy-start = (bf16[64,2048]{1,0:T(8,128)(2,1)S(1)}, bf16[64,2048]{1,0:T(8,128)(2,1)}, u32[]{:S(2)}) copy-start(bf16[64,2048]{1,0:T(8,128)(2,1)} %qry_hbm.1) | copy-start | bytes 786436
  1.6 0.9 %copy-start.1 = (bf16[32,2048]{1,0:T(8,128)(2,1)S(1)}, bf16[32,2048]{1,0:T(8,128)(2,1)}, u32[]{:S(2)}) copy-start(bf16[32,2048]{1,0:T(8,128)(2,1)} %feat.1) | copy-start | bytes 393220
  2.5 0.7 %copy-start.2 = (f32[512]{0:T(512)S(1)}, f32[512]{0:T(512)}, u32[]{:S(2)}) copy-start(f32[512]{0:T(512)} %param.5) | copy-start | bytes 6148

commit v3 on v2

--- a/solution.py
+++ b/solution.py
@@ -19,8 +19,9 @@
     (0, 0), (3, 0), (1, 0), (0, 3), (0, 1), (2, 0), (3, 3), (1, 3),
     (3, 1), (1, 1), (2, 3), (2, 1), (0, 2), (3, 2), (1, 2), (2, 2),
 )
-RELAYED = 10
-LAST_STEP = 25
+RELAYED = 6
+LAG = 3
+LAST_STEP = max(RELAYED + 7 * LAG if RELAYED else 0, 16 + 4 * LAG) + 1
 
 
 def _table(values, p):
@@ -323,7 +324,7 @@
             z_copy(first, 1, True, up, 0).start()
             z_copy(first, 1, True, down, 1).start()
 
-        pu = first - 2 * hops_up
+        pu = first - LAG * hops_up
 
         @pl.when((d != 0) & (pu >= 0) & (pu < RELAYED))
         def _():
@@ -333,7 +334,7 @@
             def _():
                 z_copy(pu, 0, False, up, 0).start()
 
-        pd = first - 2 * hops_down
+        pd = first - LAG * hops_down
 
         @pl.when((d != 0) & (pd >= 0) & (pd < RELAYED))
         def _():
@@ -343,7 +344,7 @@
             def _():
                 z_copy(pd, 1, False, down, 1).start()
 
-        pn = first - 2 * near
+        pn = first - LAG * near
 
         @pl.when((d != 0) & (pn >= RELAYED) & (pn < 16))
         def _():
@@ -552,7 +553,7 @@
         compiler_params=pltpu.CompilerParams(
             collective_id=0, has_side_effects=True, vmem_limit_bytes=40 * 1024 * 1024
         ),
-    )(features, queries, damping)
+    )(*(pltpu.with_memory_space_constraint(v, pltpu.HBM) for v in (features, queries, damping)))
 
 
 def final_kernel(fj, xhi, xlo, fi, fp, linv, damp, sc, kout, fout, sout, fit, xcat):
@@ -621,7 +622,7 @@
 
 def on_device(features, queries, damping):
     damping = damping.reshape(4, 128)
-    return tuple(finish(*gather(features, queries, damping), damping))
+    return tuple(finish(*gather(features, queries, damping), pltpu.with_memory_space_constraint(damping, pltpu.HBM)))
 
 
 def solution(mesh):

time: 67.6 us -> 64.5 us (0.954)
  local copies, waits for them, and re-layouts: 2.53 us -> 0 us
    unnamed x6 -> x0, local copies, waits for them, and re-layouts: 2.53 us -> none
    pallas_call x1, Pallas kernels: 56.5 us -> 55.7 us  [gather(): pl.pallas_call(gather_kernel, name='gather', out_shape=[jax.ShapeDtypeStr...]
where the time goes in v3:
time: 64.5 us; the launch traced here: 64.4 us
  Pallas kernels  63.8 us (99%)
    pallas_call x1, Pallas kernels, gather(): pl.pallas_call(gather_kernel, name='gather', out_shape=[jax.ShapeDtypeStr...  55.7 us
    pallas_call x1, Pallas kernels, finish(): pl.pallas_call(final_kernel, name='finish', grid=(2048 // TILE,), out_sha...  8.02 us

profile of v3, /device:TPU:16, one launch (start us, length us, event | category | flops | bytes accessed | tf_op | source)
XLA Modules:
  0.0 64.4 jit_solution(2052544751579131142)
XLA Ops:
  0.6 55.7 %gather.1 = (bf16[1024,2048]{1,0:T(8,128)(2,1)S(1)}, bf16[1024,512]{1,0:T(8,128)(2,1)S(1)}, bf16[1024,256]{1,0:T(8,128)(2,1)S(1)}, f32[256,256]{1,0:T(8,128)S(1)...) custom-call(bf16[32,2048]{1,0:T(8,128)(2,1)} %feat.1, ...), custom_call_target="tpu_custom_call" | custom-call | tf_op jit(solution)/shard_map/gather/pallas_call | solution.py:529
  56.4 8.0 %finish.1 = (f32[512,2048]{1,0:T(8,128)}, f32[512,256]{1,0:T(8,128)}, f32[64,128]{1,0:T(8,128)}) custom-call(bf16[1024,2048]{1,0:T(8,128)(2,1)S(1)} %get-tuple-element.10.fj, bf16[256,2048]{1,0:T(8,128)(2,1)S(1)} %get-tuple-element.11.xhi, bf16[256,2048]{1,0:T(8,128)(2,1)S(1)} %get-tuple-element.12.xlo, bf16[1024,512]{1,0:T(8,128)(2,1)S(1)} %get-tuple-element.13.fi, ...), custom_call_target="tpu_custom_call" | custom-call | tf_op jit(solution)/shard_map/finish/pallas_call | solution.py:601

commit v4 on v3

--- a/solution.py
+++ b/solution.py
@@ -400,13 +400,6 @@
 
         qry_copy.wait()
 
-        @pl.loop(1, 8)
-        def _(k):
-            part[lax.rem(z + k, 8)] = scores_for(lax.rem(z + k, 8))
-            rs_copy(k).start()
-
-        part[z] = scores_for(z)
-
     for t in range(12):
         plane_event(t)
         if t == 4:
@@ -438,6 +431,16 @@
         @pl.when(k == 4)
         def _():
             plane_done()
+
+        @pl.when(k >= 4)
+        def _():
+            @pl.loop(2 * k - 7, 2 * k - 5)
+            def _(q):
+                part[lax.rem(z + q, 8)] = scores_for(lax.rem(z + q, 8))
+
+                @pl.when(q < 8)
+                def _():
+                    rs_copy(q).start()
 
         panel_step(k, mat, rows, cols)
 
@@ -556,6 +559,9 @@
     )(*(pltpu.with_memory_space_constraint(v, pltpu.HBM) for v in (features, queries, damping)))
 
 
+FINISH_TILE = 512
+
+
 def final_kernel(fj, xhi, xlo, fi, fp, linv, damp, sc, kout, fout, sout, fit, xcat):
     w = lax.axis_index("wide")
     z = lax.axis_index("narrow")
@@ -582,36 +588,45 @@
         xcat[:, 512:768] = -lo
         sout[...] = sc[...]
 
-    k = nn(fit[...], fj[...]) + nn(xcat[...], jnp.concatenate([xhi[...], xlo[...], xhi[...]], axis=0))
-    row = lax.broadcasted_iota(jnp.int32, (512, TILE), 0)
-    lane = lax.broadcasted_iota(jnp.int32, (512, TILE), 1)
-    col = z * 2048 + t * TILE
-    lanes = jnp.concatenate([damp[i : i + 1, :] for i in range(4)], axis=1)
-    k = k + jnp.where((row == lane) & (col == w * 512), lanes, 0.0)
-    kout[...] = jnp.where((w * 512 + row < PIV) | (col + lane < PIV), 0.0, k)
+    tile = pl.ds(pl.multiple_of(t * FINISH_TILE, FINISH_TILE), FINISH_TILE)
+    xh = xhi[:, tile]
+    k = nn(fit[...], fj[:, tile]) + nn(xcat[...], jnp.concatenate([xh, xlo[:, tile], xh], axis=0))
+    row = w * 512 + lax.broadcasted_iota(jnp.int32, (512, FINISH_TILE), 0)
+    col = z * 2048 + t * FINISH_TILE + lax.broadcasted_iota(jnp.int32, (512, FINISH_TILE), 1)
+    kout[...] = jnp.where((row < PIV) | (col < PIV), 0.0, k)
+
+    gap = w * 512 - (z * 2048 + t * FINISH_TILE)
+    for part in range(4):
+        at = gap + part * 128
+
+        @pl.when((at >= 0) & (at < FINISH_TILE) & (w * 512 + part * 128 >= PIV))
+        def _():
+            square = kout[part * 128 : part * 128 + 128, pl.ds(pl.multiple_of(at, 128), 128)]
+            on = lax.broadcasted_iota(jnp.int32, (128, 128), 0) == lax.broadcasted_iota(jnp.int32, (128, 128), 1)
+            kout[part * 128 : part * 128 + 128, pl.ds(pl.multiple_of(at, 128), 128)] = square + jnp.where(
+                on, damp[part : part + 1, :], 0.0
+            )
 
 
 def finish(fj, fi, fp, linv, xhi, xlo, sc, damping):
+    vmem = pl.BlockSpec(memory_space=pltpu.VMEM)
+
     def whole(shape):
         return pl.BlockSpec(shape, lambda t: (0,) * len(shape))
-
-    def tiled(rows):
-        return pl.BlockSpec((rows, TILE), lambda t: (0, t))
 
     return pl.pallas_call(
         final_kernel,
         name="finish",
-        grid=(2048 // TILE,),
+        grid=(2048 // FINISH_TILE,),
         out_shape=[
             jax.ShapeDtypeStruct((512, 2048), F32),
             jax.ShapeDtypeStruct((512, PIV), F32),
             jax.ShapeDtypeStruct((64, 128), F32),
         ],
-        in_specs=[
-            tiled(SLAB), tiled(PIV), tiled(PIV),
-            whole((SLAB, 512)), whole((SLAB, PIV)), whole((PIV, PIV)), whole((4, 128)), whole((64, 128)),
+        in_specs=[vmem] * 8,
+        out_specs=[
+            pl.BlockSpec((512, FINISH_TILE), lambda t: (0, t)), whole((512, PIV)), whole((64, 128)),
         ],
-        out_specs=[tiled(512), whole((512, PIV)), whole((64, 128))],
         scratch_shapes=[
             pltpu.VMEM((512, SLAB), BF16),
             pltpu.VMEM((512, 768), BF16),

time: 64.5 us -> 64.5 us (level)
  no operation moved by 1% of the time
where the time goes in v4:
time: 64.5 us; the launch traced here: 64.3 us
  Pallas kernels  63.7 us (99%)
    pallas_call x1, Pallas kernels, gather(): pl.pallas_call(gather_kernel, name='gather', out_shape=[jax.ShapeDtypeStr...  55.8 us
    pallas_call x1, Pallas kernels, finish(): pl.pallas_call(final_kernel, name='finish', grid=(2048 // FINISH_TILE,),...  7.95 us

profile of v4, /device:TPU:16, one launch (start us, length us, event | category | flops | bytes accessed | tf_op | source)
XLA Modules:
  0.0 64.3 jit_solution(4726608710464403205)
XLA Ops:
  0.6 55.8 %gather.1 = (bf16[1024,2048]{1,0:T(8,128)(2,1)S(1)}, bf16[1024,512]{1,0:T(8,128)(2,1)S(1)}, bf16[1024,256]{1,0:T(8,128)(2,1)S(1)}, f32[256,256]{1,0:T(8,128)S(1)...) custom-call(bf16[32,2048]{1,0:T(8,128)(2,1)} %feat.1, ...), custom_call_target="tpu_custom_call" | custom-call | tf_op jit(solution)/shard_map/gather/pallas_call | solution.py:532
  56.4 7.9 %finish.1 = (f32[512,2048]{1,0:T(8,128)}, f32[512,256]{1,0:T(8,128)}, f32[64,128]{1,0:T(8,128)}) custom-call(bf16[1024,2048]{1,0:T(8,128)(2,1)S(1)} %get-tuple-element.10.fj, bf16[256,2048]{1,0:T(8,128)(2,1)S(1)} %get-tuple-element.11.xhi, bf16[256,2048]{1,0:T(8,128)(2,1)S(1)} %get-tuple-element.12.xlo, bf16[1024,512]{1,0:T(8,128)(2,1)S(1)} %get-tuple-element.13.fi, ...), custom_call_target="tpu_custom_call" | custom-call | tf_op jit(solution)/shard_map/finish/pallas_call | solution.py:617
